TPU v7x, 32 devices: a whole 2x2x4 slice. The times are simulated.
32 devices in a mesh: row: 4 (over y, x), col: 8 (over z, core).
Axes of the slice: x: 2, y: 2, z: 4, core: 2. Of those that a mesh axis runs over, the one named last changes fastest.
Arguments:
- wavefield: bfloat16 [2, 1, 8192, 8192], P(None, None, 'row', 'col'), as said below
- panel_order: int32 [16], replicated, may hold values from 0 to 15, each once
- filter_taps: float32 [11, 8192], P(None, 'col'), may hold values from -4 to 4
Outputs:
- primaries: bfloat16 [2, 1, 8192, 8192], P(None, None, 'row', 'col')
Inputs may be any that keep to these rules, and one draw needn't show every extreme that they name: Reciprocity: wavefield[c, f, s, r] = wavefield[c, f, r, s] for every part, frequency, shot and receiver.
All inputs are finite; a program needn't handle non-finite values.
Results may differ from a plain program's by a relative error of at most 0.00045.
Values may be sent and summed in bfloat16 or wider, within the bound.
A program may use at most 128 MiB of HBM per device.

v0:
```python
import math
import jax
import jax.numpy as jnp
from jax import lax
from jax.sharding import PartitionSpec as P

SIDE = 8192
PANEL = 512
STEPS = 3
TAPS = 11
FIRST_FREQUENCY = 8
NT = 1024


def spread(block, axis, holder):
    block = jnp.where(lax.axis_index(axis) == holder, block, jnp.zeros_like(block))
    return lax.psum(block, axis)


def frequency_spectrum(filter_taps, freq_count):
    lags = jnp.arange(TAPS, dtype=jnp.float32)
    omega = 2.0 * math.pi * (FIRST_FREQUENCY + jnp.arange(freq_count, dtype=jnp.float32)) / NT
    phase = omega[:, None] * lags[None, :]
    real_part = jnp.dot(jnp.cos(phase), filter_taps, precision=lax.Precision.HIGHEST)
    imag_part = -jnp.dot(jnp.sin(phase), filter_taps, precision=lax.Precision.HIGHEST)
    return (real_part, imag_part)


def local(wavefield, panel_order, filter_taps):
    freq_count = wavefield.shape[1]
    shot_block = wavefield.shape[2]
    recv_block = wavefield.shape[3]
    own_row_index = lax.axis_index("row")
    factor = 1.0 / math.sqrt(STEPS * PANEL)
    count = 2.0 * SIDE * SIDE
    local_data = jnp.sum(jnp.square(wavefield.astype(jnp.float32)), axis=(0, 2, 3))
    energy_data = lax.psum(local_data, ("row", "col"))
    totals = jnp.zeros((freq_count, shot_block, 2 * recv_block), jnp.float32)
    for panel_advance in range(STEPS):
        first_point = panel_order[panel_advance] * PANEL
        row_width = min(PANEL, shot_block)
        owner_turn = 0
        start = first_point + owner_turn * row_width
        piece = lax.dynamic_slice_in_dim(wavefield, start % shot_block, row_width, 2)
        row_pieces = spread(piece, "row", start // shot_block)
        col_pieces = []
        mirror_width = min(shot_block, recv_block)
        for owner_turn in range(max(1, shot_block // recv_block)):
            start = own_row_index * shot_block + owner_turn * mirror_width
            piece = row_pieces
            col_pieces.append(spread(piece, "col", start // recv_block))
        upper = jnp.swapaxes(jnp.concatenate(col_pieces, axis=3), 2, 3)
        left_factor = jnp.concatenate([upper[0], upper[1]], axis=2)
        right_factor = jnp.concatenate(
            [
                jnp.concatenate([row_pieces[0], row_pieces[1]], axis=2),
                jnp.concatenate([-row_pieces[1], row_pieces[0]], axis=2),
            ],
            axis=1,
        )
        totals = totals + jnp.einsum(
            "yga,yah->ygh", left_factor, right_factor, preferred_element_type=jnp.float32
        )
    mult_re = totals[:, :, :recv_block] * factor
    mult_im = totals[:, :, recv_block:] * factor
    local_mult = jnp.sum(mult_re * mult_re, axis=(1, 2)) + jnp.sum(mult_im * mult_im, axis=(1, 2))
    energy_mult = lax.psum(local_mult, ("row", "col"))
    gain = jnp.sqrt((energy_data / count + 1e-05) / (energy_mult / count + 1e-05))[:, None, None]
    spec_re, spectrum_imaginary = frequency_spectrum(filter_taps, freq_count)
    a_re = spec_re[:, None, :]
    a_im = spectrum_imaginary[:, None, :]
    sub_re = gain * (a_re * mult_re - a_im * mult_im)
    subtracted_imaginary = gain * (a_re * mult_im + a_im * mult_re)
    result = jnp.stack(
        [
            wavefield[0].astype(jnp.float32) - sub_re,
            wavefield[1].astype(jnp.float32) - subtracted_imaginary,
        ]
    )
    return result.astype(jnp.bfloat16)


def solution(mesh):
    in_specs = (P(None, None, "row", "col"), P(), P(None, "col"))
    out_specs = P(None, None, "row", "col")
    return jax.shard_map(local, mesh=mesh, in_specs=in_specs, out_specs=out_specs, check_vma=False)
```

profile of v0, /device:TPU:0, one launch (start us, length us, event | category | flops | bytes accessed | tf_op | source)
XLA Modules:
  0.0 574.6 jit_solution(4812918331580029134)
XLA Ops:
  6.5 1.4 fusion.46
  9.9 7.0 %dynamic-slice_select_fusion = (bf16[2,1,512,1024]{3,2,1,0:T(8,128)(2,1)}, bf16[2,1,512,1024]{3,2,1,0:T(8,128)(2,1)}, bf16[2,1,512,1024]{3,2,1,0:T(8,128)(2,1)}) fusion(bf16[2,1,2048,1024]{3,2,1,0:T(8,128)(2,1)} %param.3, s32[]{:T(128)S(6)} %select_n.113, pred[]{:T(512)S(6)} %eq.27, s32[]{:T(128)S(6)} %select_n.106, pred[]{:T(512)S(6)} %eq.26, ...), kind=kLoop, calls=%fused_computation.52 | loop fusion | flops 3145728 | bytes 12582927 | tf_op jit(solution)/shard_map/jit(_where)/select_n | solution.py:16
  17.2 140.8 %all-reduce.8.cloned.1.call-done = (bf16[2,1,512,1024]{3,2,1,0:T(8,128)(2,1)}, bf16[2,1,512,1024]{3,2,1,0:T(8,128)(2,1)}, bf16[2,1,512,1024]{3,2,1,0:T(8,128)(2,1)}) async-done(((bf16[2,1,512,1024]{3,2,1,0:T(8,128)(2,1)}, bf16[2,1,512,1024]{3,2,1,0:T(8,128)(2,1)}, bf16[2,1,512,1024]{3,2,1,0:T(8,128)(2,1)}), (bf16[2,1,512,1024]{3,2,1,0:T(8,128)(2,1)}, bf16[2,1,512,1024]{3,2,1,0:T(8,128)(2,1)}, ...) | async-done | bytes 6291472 | tf_op jit(solution)/shard_map/psum | solution.py:17
  158.0 4.0 broadcast_select_fusion.5
  162.0 3.5 broadcast_select_fusion.3
  166.0 8.5 %multiply_reduce_fusion = f32[]{:T(128)} fusion(bf16[2,1,2048,1024]{3,2,1,0:T(8,128)(2,1)} %param.3), kind=kLoop, calls=%fused_computation.1 | loop fusion | flops 12582911 | bytes 8388612 | tf_op jit(solution)/shard_map/reduce_sum | solution.py:36
  174.5 1.6 slice_bitcast_fusion.10
  176.1 0.7 copy-done.4
  176.8 1.6 fusion.43
  178.4 2.1 slice_bitcast_fusion.6
  180.5 239.8 %all-reduce.6.cloned.1.call-done = (bf16[2,1,512,1024]{3,2,1,0:T(8,128)(2,1)}, bf16[2,1,512,1024]{3,2,1,0:T(8,128)(2,1)}, bf16[2,1,512,1024]{3,2,1,0:T(8,128)(2,...) async-done(((bf16[2,1,512,1024]{3,2,1,0:T(8,128)(2,1)}, bf16[2,1,512,1024]{3,2,1,0:T(8,128)(2,1)}, ...) | async-done | bytes 12582928 | tf_op jit(solution)/shard_map/psum | solution.py:17
  420.4 2.7 maximum_bitcast_fusion
  423.4 1.3 copy-done.8
  424.7 0.6 copy-done.9
  425.8 0.6 slice_bitcast_fusion.3
  426.4 1.0 copy-done.6
  427.4 0.6 copy-done.7
  429.0 14.7 %fusion.13 = f32[2048,2048]{1,0:T(8,128)} fusion(bf16[1,2048,512]{1,2,0:T(8,128)(2,1)S(1)} %get-tuple-element.26, bf16[1,2048,512]{1,2,0:T(8,128)(2,1)S(1)} %get-tuple-element.25, bf16[1,512,1024]{2,1,0:T(8,128)(2,1)} %get-tuple-element.46, bf16[1,512,1024]{2,1,0:T(8,128)(2,1)} %get-tuple-element.49, bf16[1,512,1024]{2,1,0:T(8,128)(2,1)} %get-tuple-element.47), kind=kOutput, calls=%fused_computation.25 | convolution fusion | flops 8615100416 | bytes 24117248 | tf_op jit(solution)/shard_map/yga,yah->ygh/dot_general | solution.py:61
  443.8 25.3 %fusion.4 = f32[2048,2048]{1,0:T(8,128)} fusion(bf16[1,2048,512]{1,2,0:T(8,128)(2,1)S(1)} %get-tuple-element.28, bf16[1,2048,512]{1,2,0:T(8,128)(2,1)S(1)} %get-tuple-element.27, bf16[1,512,1024]{2,1,0:T(8,128)(2,1)S(1)} %copy-done.11, bf16[1,512,1024]{2,1,0:T(8,128)(2,1)S(1)} %copy-done.12, bf16[1,512,1024]{2,1,0:T(8,128)(2,1)S(1)} %copy-done.10), kind=kOutput, calls=%fused_computation.13 | convolution fusion | flops 8615100416 | bytes 24117248 | tf_op jit(solution)/shard_map/yga,yah->ygh/dot_general | solution.py:61
  469.1 29.0 %add_bitcast_fusion = f32[1,2048,2048]{2,1,0:T(8,128)} fusion(f32[2048,2048]{1,0:T(8,128)} %fusion.4, f32[2048,2048]{1,0:T(8,128)} %fusion.13, bf16[1,2048,512]{1,2,0:T(8,128)(2,1)S(1)} %get-tuple-element.24, bf16[1,2048,512]{1,2,0:T(8,128)(2,1)S(1)} %get-tuple-element.23, bf16[1,512,1024]{2,1,0:T(8,128)(2,1)S(1)} %copy-done.14, ...), kind=kOutput, calls=%fused_computation | convolution fusion | flops 8623489024 | bytes 57671680 | tf_op jit(solution)/shard_map/yga,yah->ygh/dot_general | solution.py:61
  498.1 7.5 %multiply_reduce_fusion.1 = (f32[]{:T(128)}, f32[]{:T(128)}) fusion(f32[1,2048,2048]{2,1,0:T(8,128)} %add_bitcast_fusion), kind=kLoop, calls=%fused_computation.7 | loop fusion | flops 12582910 | bytes 16777224 | tf_op jit(solution)/shard_map/reduce_sum | solution.py:66
  506.9 40.9 %all-reduce = (f32[1]{0:T(128)}, f32[1]{0:T(128)}) all-reduce(f32[1]{0:T(128)} %bitcast.1, f32[1]{0:T(128)} %bitcast.27), channel_id=1, replica_groups=mesh['row'=4,'col'=8] {'row','col'}, use_global_device_ids=true, to_apply=%region_1.0 | all-reduce | flops 2 | bytes 16 | tf_op jit(solution)/shard_map/psum | solution.py:37
  549.1 12.3 %fusion.2 = (bf16[1,1,2048,1024]{3,2,1,0:T(8,128)(2,1)S(1)}, bf16[1,1,2048,1024]{3,2,1,0:T(8,128)(2,1)}) fusion(f32[1,2048,2048]{2,1,0:T(8,128)} %add_bitcast_fusion, f32[1024]{0:T(1024)S(1)} %get-tuple-element.50, f32[1024]{0:T(1024)S(1)} %get-tuple-element.51, f32[]{:T(128)} %bitcast.28, bf16[2,1,2048,1024]{3,2,1,0:T(8,128)(2,1)} %param.3), kind=kLoop, calls=%fused_computation.9 | loop fusion | flops 29360128 | bytes 33562628 | tf_op jit(solution)/shard_map/stack | solution.py:74
  561.3 6.4 %pad_maximum_fusion = bf16[2,1,2048,1024]{3,2,1,0:T(8,128)(2,1)} fusion(bf16[1,1,2048,1024]{3,2,1,0:T(8,128)(2,1)} %get-tuple-element.19, bf16[1,1,2048,1024]{3,2,1,0:T(8,128)(2,1)S(1)} %get-tuple-element.18), kind=kLoop, calls=%fused_computation.2 | loop fusion | flops 4194304 | bytes 16777216 | tf_op jit(solution)/shard_map/stack | solution.py:74
  (37 shorter events, 2.6 us)
Async XLA Ops:
  6.5 159.0 %copy-start = (f32[11,1024]{1,0:T(8,128)S(1)}, f32[11,1024]{1,0:T(8,128)}, u32[]{:S(2)}) copy-start(f32[11,1024]{1,0:T(8,128)} %param.5) | copy-start | bytes 135172
  6.5 151.4 %all-reduce.8.cloned.1.call-start = ((), (), s32[]{:S(2)}) async-start(), calls=%async_computation.1 | async-start | bytes 12582912 | tf_op jit(solution)/shard_map/psum | solution.py:17
  16.9 403.4 %all-reduce.6.cloned.1.call-start = ((), (), s32[]{:S(2)}) async-start(), calls=%async_computation | async-start | bytes 25165824 | tf_op jit(solution)/shard_map/psum | solution.py:17
  158.0 4.0 copy-start.2
  158.0 4.0 copy-start.3
  166.0 8.5 %copy-start.5 = (bf16[2,1,512,1024]{3,2,1,0:T(8,128)(2,1)S(1)}, bf16[2,1,512,1024]{3,2,1,0:T(8,128)(2,1)}, u32[]{:S(2)}) copy-start(bf16[2,1,512,1024]{3,2,1,0:T(8,128)(2,1)} %get-tuple-element.15) | copy-start | bytes 6291460
  174.4 2.3 copy-start.4
  423.1 1.6 copy-start.8
  423.1 2.2 copy-start.9
  425.8 1.6 copy-start.6
  425.8 2.2 copy-start.7
  429.0 14.8 %copy-start.10 = (bf16[1,512,1024]{2,1,0:T(8,128)(2,1)S(1)}, bf16[1,512,1024]{2,1,0:T(8,128)(2,1)}, u32[]{:S(2)}) copy-start(bf16[1,512,1024]{2,1,0:T(8,128)(2,1)} %get-tuple-element.33) | copy-start | bytes 3145732
  429.0 14.8 %copy-start.11 = (bf16[1,512,1024]{2,1,0:T(8,128)(2,1)S(1)}, bf16[1,512,1024]{2,1,0:T(8,128)(2,1)}, u32[]{:S(2)}) copy-start(bf16[1,512,1024]{2,1,0:T(8,128)(2,1)} %get-tuple-element.34) | copy-start | bytes 3145732
  429.0 14.8 %copy-start.12 = (bf16[1,512,1024]{2,1,0:T(8,128)(2,1)S(1)}, bf16[1,512,1024]{2,1,0:T(8,128)(2,1)}, u32[]{:S(2)}) copy-start(bf16[1,512,1024]{2,1,0:T(8,128)(2,1)} %get-tuple-element.48) | copy-start | bytes 3145732
  443.8 25.3 %copy-start.13 = (bf16[1,512,1024]{2,1,0:T(8,128)(2,1)S(1)}, bf16[1,512,1024]{2,1,0:T(8,128)(2,1)}, u32[]{:S(2)}) copy-start(bf16[1,512,1024]{2,1,0:T(8,128)(2,1)} %get-tuple-element.29) | copy-start | bytes 3145732
  443.8 25.3 %copy-start.14 = (bf16[1,512,1024]{2,1,0:T(8,128)(2,1)S(1)}, bf16[1,512,1024]{2,1,0:T(8,128)(2,1)}, u32[]{:S(2)}) copy-start(bf16[1,512,1024]{2,1,0:T(8,128)(2,1)} %get-tuple-element.30) | copy-start | bytes 3145732
  561.3 6.4 %copy-start.1 = (f32[11,1024]{1,0:T(8,128)S(1)}, f32[11,1024]{1,0:T(8,128)}, u32[]{:S(2)}) copy-start(f32[11,1024]{1,0:T(8,128)} %param.5) | copy-start | bytes 135172
Sparse Core Ops, SparseCore 0:
  17.0 140.8 all-reduce.7
  165.6 254.6 all-reduce.5
where the time goes:
time: 575 us
  waiting for transfers between devices  381 us (66%)
  matrix products  69.4 us (12%)
  other arithmetic  54.4 us (9%)
  blocking collectives  40.9 us (7%)
  between operations  18.1 us (3%)
  local copies, waits for them, and re-layouts  10.8 us (2%)
    psum x2, waiting for transfers between devices, spread(): return lax.psum(block, axis)  381 us
    dot_general x3, matrix products, local(): jnp.einsum('yga,yah->ygh', left_factor, right_factor, preferred_element_t...  69 us
    psum x1, blocking collectives, local(): energy_data = lax.psum(local_data, ('row', 'col'))  40.9 us
    another operation x2, other arithmetic, local(): jnp.stack([wavefield[0].astype(jnp.float32) - sub_re, wavefield[1].astype...  18.6 us
    select_n x3, other arithmetic, spread(): jnp.where(lax.axis_index(axis) == holder, block, jnp.zeros_like(block))  14.5 us
  transfers between devices with their start and end apart: 2, of which 2 were waited for; matrix products, arithmetic and copies ran while one was open for 2% of the time, Pallas kernels for 0%

commit v1 on v0

--- a/solution.py
+++ b/solution.py
@@ -34,7 +34,7 @@
     factor = 1.0 / math.sqrt(STEPS * PANEL)
     count = 2.0 * SIDE * SIDE
     local_data = jnp.sum(jnp.square(wavefield.astype(jnp.float32)), axis=(0, 2, 3))
-    energy_data = lax.psum(local_data, ("row", "col"))
+    energy_data = lax.psum(lax.psum(local_data, "col"), "row")
     totals = jnp.zeros((freq_count, shot_block, 2 * recv_block), jnp.float32)
     for panel_advance in range(STEPS):
         first_point = panel_order[panel_advance] * PANEL

time: 575 us -> 575 us (level)
  waiting for transfers between devices: 381 us -> 352 us
  blocking collectives: 40.9 us -> 68.4 us
    psum x2, waiting for transfers between devices: 381 us -> 352 us  [spread(): return lax.psum(block, axis)]
    psum x1 -> x3, blocking collectives: 40.9 us -> 68.4 us  [the longest x1 40.9 us: local(): energy_mult = lax.psum(local_mult, ('row', 'col'))]
  transfers between devices with their start and end apart: 2 -> 2, of which waited for: 2 -> 2; matrix products, arithmetic and copies ran while one was open for 2% -> 3% of each run, Pallas kernels for 0% -> 0%
where the time goes in v1:
time: 575 us; the launch traced here: 574 us
  waiting for transfers between devices  352 us (61%)
  matrix products  69.5 us (12%)
  blocking collectives  68.4 us (12%)
  other arithmetic  54.1 us (9%)
  between operations  18.5 us (3%)
  local copies, waits for them, and re-layouts  11.6 us (2%)
    psum x2, waiting for transfers between devices, spread(): return lax.psum(block, axis)  352 us
    dot_general x3, matrix products, local(): jnp.einsum('yga,yah->ygh', left_factor, right_factor, preferred_element_t...  69.1 us
    psum x1, blocking collectives, local(): energy_mult = lax.psum(local_mult, ('row', 'col'))  40.9 us
    psum x2, blocking collectives, local(): energy_data = lax.psum(lax.psum(local_data, 'col'), 'row')  27.5 us
    another operation x2, other arithmetic, local(): jnp.stack([wavefield[0].astype(jnp.float32) - sub_re, wavefield[1].astype...  18.6 us
    select_n x3, other arithmetic, spread(): jnp.where(lax.axis_index(axis) == holder, block, jnp.zeros_like(block))  14.4 us
  transfers between devices with their start and end apart: 2, of which 2 were waited for; matrix products, arithmetic and copies ran while one was open for 3% of the time, Pallas kernels for 0%

profile of v1, /device:TPU:0, one launch (start us, length us, event | category | flops | bytes accessed | tf_op | source)
XLA Modules:
  0.0 574.4 jit_solution(11574500970910910275)
XLA Ops:
  6.5 1.4 fusion.46
  10.0 7.0 %dynamic-slice_select_fusion = (bf16[2,1,512,1024]{3,2,1,0:T(8,128)(2,1)}, bf16[2,1,512,1024]{3,2,1,0:T(8,128)(2,1)}, bf16[2,1,512,1024]{3,2,1,0:T(8,128)(2,1)}) fusion(bf16[2,1,2048,1024]{3,2,1,0:T(8,128)(2,1)} %param.3, s32[]{:T(128)S(6)} %select_n.113, pred[]{:T(512)S(6)} %eq.27, s32[]{:T(128)S(6)} %select_n.106, pred[]{:T(512)S(6)} %eq.26, ...), kind=kLoop, calls=%fused_computation.52 | loop fusion | flops 3145728 | bytes 12582927 | tf_op jit(solution)/shard_map/jit(_where)/select_n | solution.py:16
  17.0 141.0 %all-reduce.7.cloned.1.call-done = (bf16[2,1,512,1024]{3,2,1,0:T(8,128)(2,1)}, bf16[2,1,512,1024]{3,2,1,0:T(8,128)(2,1)}, bf16[2,1,512,1024]{3,2,1,0:T(8,128)(2,1)}) async-done(((bf16[2,1,512,1024]{3,2,1,0:T(8,128)(2,1)}, bf16[2,1,512,1024]{3,2,1,0:T(8,128)(2,1)}, bf16[2,1,512,1024]{3,2,1,0:T(8,128)(2,1)}), (bf16[2,1,512,1024]{3,2,1,0:T(8,128)(2,1)}, bf16[2,1,512,1024]{3,2,1,0:T(8,128)(2,1)}, ...) | async-done | bytes 6291472 | tf_op jit(solution)/shard_map/psum | solution.py:17
  158.0 4.0 broadcast_select_fusion.5
  162.0 3.4 broadcast_select_fusion.3
  165.5 8.3 %multiply_reduce_fusion = f32[]{:T(128)} fusion(bf16[2,1,2048,1024]{3,2,1,0:T(8,128)(2,1)} %param.3), kind=kLoop, calls=%fused_computation.1 | loop fusion | flops 12582911 | bytes 8388612 | tf_op jit(solution)/shard_map/reduce_sum | solution.py:36
  173.8 17.7 %psum.84 = f32[1]{0:T(128)} all-reduce(f32[1]{0:T(128)} %bitcast.1), channel_id=1, replica_groups=mesh['row'=4,'col'=8] {'col'}, use_global_device_ids=true, to_apply=%region_1.0 | all-reduce | flops 1 | bytes 8 | tf_op jit(solution)/shard_map/psum | solution.py:37
  191.5 9.8 %psum.85 = f32[1]{0:T(128)} all-reduce(f32[1]{0:T(128)} %psum.84), channel_id=1, replica_groups=mesh['row'=4,'col'=8] {'row'}, use_global_device_ids=true, to_apply=%region_2.0 | all-reduce | flops 1 | bytes 8 | tf_op jit(solution)/shard_map/psum | solution.py:37
  202.7 3.0 slice_bitcast_fusion.10
  205.7 1.5 fusion.43
  207.2 2.1 slice_bitcast_fusion.6
  209.3 211.3 %all-reduce.5.cloned.1.call-done = (bf16[2,1,512,1024]{3,2,1,0:T(8,128)(2,1)}, bf16[2,1,512,1024]{3,2,1,0:T(8,128)(2,1)}, bf16[2,1,512,1024]{3,2,1,0:T(8,128)(2,...) async-done(((bf16[2,1,512,1024]{3,2,1,0:T(8,128)(2,1)}, bf16[2,1,512,1024]{3,2,1,0:T(8,128)(2,1)}, ...) | async-done | bytes 12582928 | tf_op jit(solution)/shard_map/psum | solution.py:17
  420.6 2.7 maximum_bitcast_fusion
  423.7 1.3 copy-done.8
  425.0 0.6 copy-done.9
  426.6 1.0 copy-done.6
  427.6 0.6 copy-done.7
  429.3 14.8 %fusion.13 = f32[2048,2048]{1,0:T(8,128)} fusion(bf16[1,2048,512]{1,2,0:T(8,128)(2,1)S(1)} %get-tuple-element.24, bf16[1,2048,512]{1,2,0:T(8,128)(2,1)S(1)} %get-tuple-element.23, bf16[1,512,1024]{2,1,0:T(8,128)(2,1)} %get-tuple-element.44, bf16[1,512,1024]{2,1,0:T(8,128)(2,1)} %get-tuple-element.47, bf16[1,512,1024]{2,1,0:T(8,128)(2,1)} %get-tuple-element.45), kind=kOutput, calls=%fused_computation.25 | convolution fusion | flops 8615100416 | bytes 24117248 | tf_op jit(solution)/shard_map/yga,yah->ygh/dot_general | solution.py:61
  444.1 25.4 %fusion.4 = f32[2048,2048]{1,0:T(8,128)} fusion(bf16[1,2048,512]{1,2,0:T(8,128)(2,1)S(1)} %get-tuple-element.26, bf16[1,2048,512]{1,2,0:T(8,128)(2,1)S(1)} %get-tuple-element.25, bf16[1,512,1024]{2,1,0:T(8,128)(2,1)S(1)} %copy-done.11, bf16[1,512,1024]{2,1,0:T(8,128)(2,1)S(1)} %copy-done.12, bf16[1,512,1024]{2,1,0:T(8,128)(2,1)S(1)} %copy-done.10), kind=kOutput, calls=%fused_computation.13 | convolution fusion | flops 8615100416 | bytes 24117248 | tf_op jit(solution)/shard_map/yga,yah->ygh/dot_general | solution.py:61
  469.5 28.9 %add_bitcast_fusion = f32[1,2048,2048]{2,1,0:T(8,128)} fusion(f32[2048,2048]{1,0:T(8,128)} %fusion.4, f32[2048,2048]{1,0:T(8,128)} %fusion.13, bf16[1,2048,512]{1,2,0:T(8,128)(2,1)S(1)} %get-tuple-element.22, bf16[1,2048,512]{1,2,0:T(8,128)(2,1)S(1)} %get-tuple-element.21, bf16[1,512,1024]{2,1,0:T(8,128)(2,1)S(1)} %copy-done.14, ...), kind=kOutput, calls=%fused_computation | convolution fusion | flops 8623489024 | bytes 57671680 | tf_op jit(solution)/shard_map/yga,yah->ygh/dot_general | solution.py:61
  498.4 7.6 %multiply_reduce_fusion.1 = (f32[]{:T(128)}, f32[]{:T(128)}) fusion(f32[1,2048,2048]{2,1,0:T(8,128)} %add_bitcast_fusion), kind=kLoop, calls=%fused_computation.7 | loop fusion | flops 12582910 | bytes 16777224 | tf_op jit(solution)/shard_map/reduce_sum | solution.py:66
  507.3 40.9 %psum.95 = f32[1]{0:T(128)} all-reduce(f32[1]{0:T(128)} %bitcast.27), channel_id=1, replica_groups=mesh['row'=4,'col'=8] {'row','col'}, use_global_device_ids=true, to_apply=%region_14.15 | all-reduce | flops 1 | bytes 8 | tf_op jit(solution)/shard_map/psum | solution.py:67
  548.9 12.3 %fusion.2 = (bf16[1,1,2048,1024]{3,2,1,0:T(8,128)(2,1)S(1)}, bf16[1,1,2048,1024]{3,2,1,0:T(8,128)(2,1)}) fusion(f32[1,2048,2048]{2,1,0:T(8,128)} %add_bitcast_fusion, f32[1024]{0:T(1024)S(1)} %get-tuple-element.48, f32[1024]{0:T(1024)S(1)} %get-tuple-element.49, f32[]{:T(128)} %bitcast.28, bf16[2,1,2048,1024]{3,2,1,0:T(8,128)(2,1)} %param.3), kind=kLoop, calls=%fused_computation.9 | loop fusion | flops 29360128 | bytes 33562628 | tf_op jit(solution)/shard_map/stack | solution.py:74
  561.1 6.4 %pad_maximum_fusion = bf16[2,1,2048,1024]{3,2,1,0:T(8,128)(2,1)} fusion(bf16[1,1,2048,1024]{3,2,1,0:T(8,128)(2,1)} %get-tuple-element.17, bf16[1,1,2048,1024]{3,2,1,0:T(8,128)(2,1)S(1)} %get-tuple-element.16), kind=kLoop, calls=%fused_computation.2 | loop fusion | flops 4194304 | bytes 16777216 | tf_op jit(solution)/shard_map/stack | solution.py:74
  (39 shorter events, 3.0 us)
Async XLA Ops:
  6.5 195.6 %copy-start = (f32[11,1024]{1,0:T(8,128)S(1)}, f32[11,1024]{1,0:T(8,128)}, u32[]{:S(2)}) copy-start(f32[11,1024]{1,0:T(8,128)} %param.5) | copy-start | bytes 135172
  6.5 151.5 %all-reduce.7.cloned.1.call-start = ((), (), s32[]{:S(2)}) async-start(), calls=%async_computation.1 | async-start | bytes 12582912 | tf_op jit(solution)/shard_map/psum | solution.py:17
  16.9 403.7 %all-reduce.5.cloned.1.call-start = ((), (), s32[]{:S(2)}) async-start(), calls=%async_computation | async-start | bytes 25165824 | tf_op jit(solution)/shard_map/psum | solution.py:17
  158.0 4.0 copy-start.2
  158.0 4.1 copy-start.3
  201.3 4.4 copy-start.4
  201.3 4.4 copy-start.5
  423.4 1.6 copy-start.8
  423.4 2.2 copy-start.9
  426.0 1.6 copy-start.6
  426.0 2.2 copy-start.7
  429.3 14.8 %copy-start.10 = (bf16[1,512,1024]{2,1,0:T(8,128)(2,1)S(1)}, bf16[1,512,1024]{2,1,0:T(8,128)(2,1)}, u32[]{:S(2)}) copy-start(bf16[1,512,1024]{2,1,0:T(8,128)(2,1)} %get-tuple-element.31) | copy-start | bytes 3145732
  429.3 14.8 %copy-start.11 = (bf16[1,512,1024]{2,1,0:T(8,128)(2,1)S(1)}, bf16[1,512,1024]{2,1,0:T(8,128)(2,1)}, u32[]{:S(2)}) copy-start(bf16[1,512,1024]{2,1,0:T(8,128)(2,1)} %get-tuple-element.32) | copy-start | bytes 3145732
  429.3 14.8 %copy-start.12 = (bf16[1,512,1024]{2,1,0:T(8,128)(2,1)S(1)}, bf16[1,512,1024]{2,1,0:T(8,128)(2,1)}, u32[]{:S(2)}) copy-start(bf16[1,512,1024]{2,1,0:T(8,128)(2,1)} %get-tuple-element.46) | copy-start | bytes 3145732
  444.1 25.4 %copy-start.13 = (bf16[1,512,1024]{2,1,0:T(8,128)(2,1)S(1)}, bf16[1,512,1024]{2,1,0:T(8,128)(2,1)}, u32[]{:S(2)}) copy-start(bf16[1,512,1024]{2,1,0:T(8,128)(2,1)} %get-tuple-element.27) | copy-start | bytes 3145732
  444.1 25.4 %copy-start.14 = (bf16[1,512,1024]{2,1,0:T(8,128)(2,1)S(1)}, bf16[1,512,1024]{2,1,0:T(8,128)(2,1)}, u32[]{:S(2)}) copy-start(bf16[1,512,1024]{2,1,0:T(8,128)(2,1)} %get-tuple-element.28) | copy-start | bytes 3145732
  561.1 6.4 %copy-start.1 = (f32[11,1024]{1,0:T(8,128)S(1)}, f32[11,1024]{1,0:T(8,128)}, u32[]{:S(2)}) copy-start(f32[11,1024]{1,0:T(8,128)} %param.5) | copy-start | bytes 135172
Sparse Core Ops, SparseCore 0:
  17.1 140.8 all-reduce.6
  165.6 254.9 all-reduce.4
